TPU v7x, 32 devices: a whole 2x2x4 slice. The times are simulated.
32 devices in a mesh: clips: 2 (over y), seq: 8 (over z, x), mp: 2 (over core).
Axes of the slice: x: 2, y: 2, z: 4, core: 2. Of those that a mesh axis runs over, the one named last changes fastest.
Arguments:
- queries: bfloat16 [12, 4096, 128], P('mp', ('clips', 'seq')), parts along dimension 1, may hold values from -6 to 6
- keys: bfloat16 [12, 4096, 128], P('mp', ('clips', 'seq')), parts along dimension 1, may hold values from -6 to 6
- values: bfloat16 [12, 4096, 128], P('mp', ('clips', 'seq')), parts along dimension 1, may hold values from -12 to 12
- out_grad: bfloat16 [12, 4096, 128], P('mp', ('clips', 'seq')), parts along dimension 1, may hold values from -12 to 12
- tile_lists: int32 [12, 8, 4], P('mp'), may hold values from -1 to 7, as said below
Outputs:
- attn_out: bfloat16 [12, 4096, 128], P('mp', ('clips', 'seq')), parts along dimension 1
- query_grad: bfloat16 [12, 4096, 128], P('mp', ('clips', 'seq')), parts along dimension 1
- key_grad: bfloat16 [12, 4096, 128], P('mp', ('clips', 'seq')), parts along dimension 1
- value_grad: bfloat16 [12, 4096, 128], P('mp', ('clips', 'seq')), parts along dimension 1
There are 2 independent parts, one for each index of `clips`. A program takes and returns all parts, laid end to end along the dimension named above; an argument that names none is the same for every part. Nothing has to cross between parts.
Inputs may be any that keep to these rules, and one draw needn't show every extreme that they name: `tile_lists`: tile ids count (time + row) * 8 + column over a grid of 1 x 1 x 8 tiles. Entry 0 of the list of head h and query tile q is q itself; the further entries name distinct tiles that share a face with q inside the grid, filled entries first and -1 in empty ones. For every tile and each of its six face directions, at most 3 heads of each group of 6 consecutive heads name that neighbour.
All inputs are finite; a program needn't handle non-finite values.
Results may differ from a plain program's by a relative error of at most 0.0067.
Values may be sent and summed in bfloat16 or wider, within the bound.
A program may use at most 64 MiB of HBM per device.

v0:
```python
import jax
import jax.numpy as jnp
from jax import lax
from jax.sharding import PartitionSpec as P

HCAP = 3
GX = 8


def passed_along(block, axis, distance):
    devices = range(lax.axis_size(axis))
    route = [(i - distance, i) for i in devices if i - distance in devices]
    return lax.ppermute(block, axis, route)


def direction_offsets(tile_count):
    row_tiles = min(4, tile_count // 8)
    layer_size = GX * row_tiles
    result = [1, -1]
    if row_tiles > 1:
        result = result + [GX, -GX]
    if tile_count // layer_size > 1:
        result = result + [layer_size, -layer_size]
    return result


def heads_naming(tile_lists, reader, named, tile_count):
    inside = (reader >= 0) & (reader < tile_count)
    reader_lists = lax.dynamic_index_in_dim(
        tile_lists, jnp.clip(reader, 0, tile_count - 1), 1, keepdims=False
    )
    return inside & jnp.any(reader_lists == named, axis=1)


def packing(head_mask):
    position = jnp.cumsum(head_mask.astype(jnp.int32)) - 1
    slot_ids = jnp.arange(HCAP, dtype=jnp.int32)
    return (head_mask[None, :] & (position[None, :] == slot_ids[:, None])).astype(jnp.bfloat16)


def pack_heads(placer, stacked):
    return jnp.einsum("ch,xhtd->xctd", placer, stacked, preferred_element_type=jnp.float32).astype(
        jnp.bfloat16
    )


def unpack_heads(placer, packed):
    return jnp.einsum("ch,xctd->xhtd", placer, packed, preferred_element_type=jnp.float32).astype(
        jnp.bfloat16
    )


def send_keys_used(key_value, send_placer, recv_placer, offset):
    packed = passed_along(pack_heads(send_placer, key_value), "seq", -offset)
    return unpack_heads(recv_placer, packed)


def send_grads_used(gradients, send_placer, recv_placer, offset):
    packed = passed_along(pack_heads(recv_placer, gradients), "seq", offset)
    return unpack_heads(send_placer, packed)


def per_device(queries, keys, values, out_grad, tile_lists):
    heads_here = queries.shape[0]
    head_width = queries.shape[2]
    tile_count = lax.axis_size("seq")
    own_tile = lax.axis_index("seq")
    offsets = direction_offsets(tile_count)
    score_scale = head_width ** (-0.5)
    own_lists = lax.dynamic_index_in_dim(tile_lists, own_tile, 1, keepdims=False)
    live_slots = own_lists >= 0
    key_value = jnp.stack([keys, values])
    fetched = [key_value]
    placers = []
    for offset in offsets:
        send_placer = packing(heads_naming(tile_lists, own_tile - offset, own_tile, tile_count))
        recv_placer = packing(heads_naming(tile_lists, own_tile, own_tile + offset, tile_count))
        placers.append((send_placer, recv_placer))
        fetched.append(send_keys_used(key_value, send_placer, recv_placer, offset))
    candidate_ids = [own_tile] + [own_tile + offset for offset in offsets]
    chooser = jnp.stack(
        [live_slots & (own_lists == candidate) for candidate in candidate_ids], axis=-1
    ).astype(jnp.bfloat16)
    candidates = jnp.stack(fetched)

    def attend(block_index):
        first_head = block_index * 2
        query_block = lax.dynamic_slice_in_dim(queries, first_head, 2, 0)
        grad_block = lax.dynamic_slice_in_dim(out_grad, first_head, 2, 0)
        chooser_block = lax.dynamic_slice_in_dim(chooser, first_head, 2, 0)
        live_block = lax.dynamic_slice_in_dim(live_slots, first_head, 2, 0)
        candidates_block = lax.dynamic_slice_in_dim(candidates, first_head, 2, 2)
        key_chosen = jnp.einsum(
            "hjc,chtd->hjtd",
            chooser_block,
            candidates_block[:, 0],
            preferred_element_type=jnp.float32,
        ).astype(jnp.bfloat16)
        value_chosen = jnp.einsum(
            "hjc,chtd->hjtd",
            chooser_block,
            candidates_block[:, 1],
            preferred_element_type=jnp.float32,
        ).astype(jnp.bfloat16)
        scores = (
            jnp.einsum(
                "hid,hjtd->hijt", query_block, key_chosen, preferred_element_type=jnp.float32
            )
            * score_scale
        )
        scores = jnp.where(live_block[:, None, :, None], scores, -jnp.inf)
        row_max = jnp.max(scores, axis=(2, 3), keepdims=True)
        weights = jnp.exp(scores - row_max)
        probs = weights / jnp.sum(weights, axis=(2, 3), keepdims=True)
        probs_low = probs.astype(jnp.bfloat16)
        attention = jnp.einsum(
            "hijt,hjtd->hid", probs_low, value_chosen, preferred_element_type=jnp.float32
        ).astype(jnp.bfloat16)
        prob_grad = jnp.einsum(
            "hid,hjtd->hijt", grad_block, value_chosen, preferred_element_type=jnp.float32
        )
        delta = jnp.sum(probs * prob_grad, axis=(2, 3), keepdims=True)
        score_grad = (probs * (prob_grad - delta)).astype(jnp.bfloat16)
        query_result = (
            jnp.einsum("hijt,hjtd->hid", score_grad, key_chosen, preferred_element_type=jnp.float32)
            * score_scale
        ).astype(jnp.bfloat16)
        key_part = (
            jnp.einsum(
                "hijt,hid->hjtd", score_grad, query_block, preferred_element_type=jnp.float32
            )
            * score_scale
        ).astype(jnp.bfloat16)
        value_part = jnp.einsum(
            "hijt,hid->hjtd", probs_low, grad_block, preferred_element_type=jnp.float32
        ).astype(jnp.bfloat16)
        return (attention, query_result, key_part, value_part)

    results = lax.map(attend, jnp.arange(heads_here // 2, dtype=jnp.int32))
    attn_out = results[0].reshape(queries.shape)
    query_grad = results[1].reshape(queries.shape)
    key_part = results[2].reshape((heads_here,) + results[2].shape[2:])
    value_part = results[3].reshape((heads_here,) + results[3].shape[2:])
    key_back = jnp.einsum(
        "hjc,hjtd->chtd", chooser, key_part, preferred_element_type=jnp.float32
    ).astype(jnp.bfloat16)
    value_back = jnp.einsum(
        "hjc,hjtd->chtd", chooser, value_part, preferred_element_type=jnp.float32
    ).astype(jnp.bfloat16)
    returned_terms = jnp.stack([key_back, value_back], axis=1)
    total = returned_terms[0].astype(jnp.float32)
    for number, offset in enumerate(offsets):
        arrived = send_grads_used(
            returned_terms[number + 1], placers[number][0], placers[number][1], offset
        )
        total = total + arrived.astype(jnp.float32)
    return (attn_out, query_grad, total[0].astype(jnp.bfloat16), total[1].astype(jnp.bfloat16))


def solution(mesh):
    placed = (
        P("mp", ("clips", "seq"), None),
        P("mp", ("clips", "seq"), None),
        P("mp", ("clips", "seq"), None),
        P("mp", ("clips", "seq"), None),
        P("mp", None, None),
    )
    return jax.shard_map(
        per_device,
        mesh=mesh,
        in_specs=placed,
        out_specs=(
            P("mp", ("clips", "seq"), None),
            P("mp", ("clips", "seq"), None),
            P("mp", ("clips", "seq"), None),
            P("mp", ("clips", "seq"), None),
        ),
        check_vma=False,
    )
```

profile of v0, /device:TPU:18, one launch (start us, length us, event | category | flops | bytes accessed | tf_op | source)
XLA Modules:
  0.0 110.8 jit_solution(8116822144961996906)
XLA Ops:
  0.6 0.9 constant_dynamic-slice_fusion.6
  2.1 1.7 %copy_bitcast_fusion.4 = (bf16[1,6,256,128]{3,1,2,0:T(8,128)(2,1)S(1)}, bf16[1,6,256,128]{3,1,2,0:T(8,128)(2,1)S(1)}) fusion(bf16[6,256,128]{2,1,0:T(8,128)(2,1)} %param.9, bf16[6,256,128]{2,1,0:T(8,128)(2,1)} %param.8), kind=kLoop, calls=%fused_computation.89 | loop fusion | bytes 1572864 | tf_op jit(solution)/shard_map/stack | solution.py:72
  3.7 0.5 fusion.55
  4.2 3.5 %collective-permute-start.1 = (bf16[2,3,256,128]{3,1,2,0:T(4,128)(2,1)S(1)}, bf16[2,3,256,128]{3,1,2,0:T(4,128)(2,1)S(1)}, u32[]{:S(2)}, u32[]{:S(2)}) collective-permute-start(bf16[2,3,256,128]{3,1,2,0:T(4,128)(2,1)S(1)} %fusion.55), channel_id=1, source_target_pairs={{0,2},{2,4},{4,6},{6,8},{8,10},{10,12},{12,14},{1,3},{3,5},{5,7},{... | collective-permute-start | bytes 1179656 | tf_op jit(solution)/shard_map/ppermute | solution.py:13
  8.5 0.5 fusion.54
  8.9 2.4 %collective-permute-start = (bf16[2,3,256,128]{3,1,2,0:T(4,128)(2,1)S(1)}, bf16[2,3,256,128]{3,1,2,0:T(4,128)(2,1)S(1)}, u32[]{:S(2)}, u32[]{:S(2)}) collective-permute-start(bf16[2,3,256,128]{3,1,2,0:T(4,128)(2,1)S(1)} %fusion.54), channel_id=1, source_target_pairs={{2,0},{4,2},{6,4},{8,6},{10,8},{12,10},{14,12},{3,1},{5,3},{7,5},{... | collective-permute-start | bytes 1179656 | tf_op jit(solution)/shard_map/ppermute | solution.py:13
  11.8 1.2 %fusion.62 = bf16[1,2,6,256,128]{4,2,3,1,0:T(8,128)(2,1)} fusion(bf16[1,6,256,128]{3,1,2,0:T(8,128)(2,1)S(1)} %get-tuple-element.156, bf16[1,6,256,128]{3,1,2,0:T(8,128)(2,1)S(1)} %get-tuple-element.157), kind=kLoop, calls=%fused_computation.93 | loop fusion | flops 393216 | bytes 1572864 | tf_op jit(solution)/shard_map/stack | solution.py:84
  13.4 0.6 fusion.86
  14.2 16.8 %collective-permute-done.1 = bf16[2,3,256,128]{3,1,2,0:T(4,128)(2,1)S(1)} collective-permute-done((bf16[2,3,256,128]{3,1,2,0:T(4,128)(2,1)S(1)}, bf16[2,3,256,128]{3,1,2,0:T(4,128)(2,1)S(1)}, u32[]{:S(2)}, u32[]{:S(2)}) %collective-permute-start.1) | collective-permute-done | bytes 393248 | tf_op jit(solution)/shard_map/ppermute | solution.py:13
  31.0 0.5 fusion.53
  31.5 0.5 fusion.52
  32.0 0.8 pad_maximum_fusion
  32.8 0.5 iota.10
  33.4 39.8 %while.16 = (s32[]{:T(128)}, bf16[3,2,256,128]{3,2,1,0:T(8,128)(2,1)}, bf16[3,2,256,128]{3,2,1,0:T(8,128)(2,1)}, bf16[3,2,4,256,128]{4,3,2,1,0:T(8,128)(2,1)}, b...) while((s32[]{:T(128)}, ...), condition=%wide.region_12.13_spmd, body=%wide.region_8.12_spmd.sunk | while | flops 825686528 | bytes 28868708 | solution.py:139
  33.4 1.2 %dynamic_slice.82 = s32[1]{0:T(128)} dynamic-slice(s32[3]{0:T(128)} %get-tuple-element.274, s32[]{:T(128)S(6)} %copy.163), dynamic_slice_sizes={1} | dynamic-slice | bytes 12 | tf_op jit(solution)/shard_map/while/body/jit(dynamic_index_in_dim)/dynamic_slice | solution.py:139
  35.1 0.6 constant_dynamic-slice_fusion.11
  35.7 0.7 copy.153
  36.4 0.8 constant_dynamic-slice_fusion.10
  37.2 0.7 convolution_convert_fusion.13
  38.0 0.7 convolution_convert_fusion.14
  39.1 0.5 fusion.120
  39.6 1.5 %fusion.121 = bf16[3,2,256,128]{3,2,1,0:T(8,128)(2,1)} fusion(bf16[3,2,256,128]{3,2,1,0:T(8,128)(2,1)} %get-tuple-element.254, s32[]{:T(128)S(6)} %copy.163, bf16[2,4,256,128]{3,1,2,0:T(4,128)(2,1)S(1)} %convolution_convert_fusion.13, f32[2,256,4,256]{1,3,2,0:T(8,128)S(1)} %get-tuple-element.233, f32[2,256]{1,0:T(2,128)S(1)} %fusion.120, ...), kind=kOutput, calls=%fused_computation.24.clone.1 | convolution fusion | flops 136904704 | bytes 2756620 | tf_op jit(solution)/shard_map/while/body/eval_jaxpr/hijt,hjtd->hid/dot_general | solution.py:116
  41.2 1.5 %fusion.124 = bf16[3,2,4,256,128]{4,3,2,1,0:T(8,128)(2,1)} fusion(bf16[3,2,4,256,128]{4,3,2,1,0:T(8,128)(2,1)} %get-tuple-element.257, s32[]{:T(128)S(6)} %copy.163, bf16[6,256,128]{2,1,0:T(8,128)(2,1)S(1)} %copy-done.19, s32[]{:T(128)S(6)} %select_n.52, f32[2,256,4,256]{1,3,2,0:T(8,128)S(1)} %get-tuple-element.233, f32[2,256]{1,0:T(2,128)S(1)} %fusion.120, ...), kind=kOutput, calls=%fused_computation.15.clone.1 | convolution fusion | flops 137101312 | bytes 2757128 | tf_op jit(solution)/shard_map/while/body/eval_jaxpr/hijt,hid->hjtd/dot_general | solution.py:134
  42.6 0.8 multiply_reduce_fusion.2
  43.4 0.8 multiply_convert_fusion.2
  44.2 1.2 %fusion.122 = bf16[3,2,256,128]{3,2,1,0:T(8,128)(2,1)} fusion(bf16[3,2,256,128]{3,2,1,0:T(8,128)(2,1)} %get-tuple-element.255, s32[]{:T(128)S(6)} %copy.163, bf16[2,256,4,256]{1,3,2,0:T(8,128)(2,1)S(1)} %multiply_convert_fusion.2, bf16[2,4,256,128]{3,1,2,0:T(4,128)(2,1)S(1)} %convolution_convert_fusion.14), kind=kOutput, calls=%fused_computation.22.clone.1 | convolution fusion | flops 134348800 | bytes 1703940 | tf_op jit(solution)/shard_map/while/body/eval_jaxpr/hijt,hjtd->hid/dot_general | solution.py:125
  45.4 1.2 %fusion.123 = bf16[3,2,4,256,128]{4,3,2,1,0:T(8,128)(2,1)} fusion(bf16[3,2,4,256,128]{4,3,2,1,0:T(8,128)(2,1)} %get-tuple-element.256, s32[]{:T(128)S(6)} %copy.163, bf16[2,256,4,256]{1,3,2,0:T(8,128)(2,1)S(1)} %multiply_convert_fusion.2, bf16[6,256,128]{2,1,0:T(8,128)(2,1)S(1)} %get-tuple-element.276, s32[]{:T(128)S(6)} %select_n.52), kind=kOutput, calls=%fused_computation.13.clone.1 | convolution fusion | flops 134742016 | bytes 1703944 | tf_op jit(solution)/shard_map/while/body/eval_jaxpr/hijt,hid->hjtd/dot_general | solution.py:129
  46.6 1.2 %dynamic_slice.82 = s32[1]{0:T(128)} dynamic-slice(s32[3]{0:T(128)} %get-tuple-element.274, s32[]{:T(128)S(6)} %copy.163), dynamic_slice_sizes={1} | dynamic-slice | bytes 12 | tf_op jit(solution)/shard_map/while/body/jit(dynamic_index_in_dim)/dynamic_slice | solution.py:139
  48.4 0.6 constant_dynamic-slice_fusion.11
  49.0 0.7 copy.153
  49.7 0.8 constant_dynamic-slice_fusion.10
  50.5 0.7 convolution_convert_fusion.13
  51.2 0.7 convolution_convert_fusion.14
  52.4 0.5 fusion.120
  52.9 1.5 %fusion.121 = bf16[3,2,256,128]{3,2,1,0:T(8,128)(2,1)} fusion(bf16[3,2,256,128]{3,2,1,0:T(8,128)(2,1)} %get-tuple-element.254, s32[]{:T(128)S(6)} %copy.163, bf16[2,4,256,128]{3,1,2,0:T(4,128)(2,1)S(1)} %convolution_convert_fusion.13, f32[2,256,4,256]{1,3,2,0:T(8,128)S(1)} %get-tuple-element.233, f32[2,256]{1,0:T(2,128)S(1)} %fusion.120, ...), kind=kOutput, calls=%fused_computation.24.clone.1 | convolution fusion | flops 136904704 | bytes 2756620 | tf_op jit(solution)/shard_map/while/body/eval_jaxpr/hijt,hjtd->hid/dot_general | solution.py:116
  54.4 1.5 %fusion.124 = bf16[3,2,4,256,128]{4,3,2,1,0:T(8,128)(2,1)} fusion(bf16[3,2,4,256,128]{4,3,2,1,0:T(8,128)(2,1)} %get-tuple-element.257, s32[]{:T(128)S(6)} %copy.163, bf16[6,256,128]{2,1,0:T(8,128)(2,1)S(1)} %copy-done.19, s32[]{:T(128)S(6)} %select_n.52, f32[2,256,4,256]{1,3,2,0:T(8,128)S(1)} %get-tuple-element.233, f32[2,256]{1,0:T(2,128)S(1)} %fusion.120, ...), kind=kOutput, calls=%fused_computation.15.clone.1 | convolution fusion | flops 137101312 | bytes 2757128 | tf_op jit(solution)/shard_map/while/body/eval_jaxpr/hijt,hid->hjtd/dot_general | solution.py:134
  55.9 0.8 multiply_reduce_fusion.2
  56.7 0.8 multiply_convert_fusion.2
  57.5 1.2 %fusion.122 = bf16[3,2,256,128]{3,2,1,0:T(8,128)(2,1)} fusion(bf16[3,2,256,128]{3,2,1,0:T(8,128)(2,1)} %get-tuple-element.255, s32[]{:T(128)S(6)} %copy.163, bf16[2,256,4,256]{1,3,2,0:T(8,128)(2,1)S(1)} %multiply_convert_fusion.2, bf16[2,4,256,128]{3,1,2,0:T(4,128)(2,1)S(1)} %convolution_convert_fusion.14), kind=kOutput, calls=%fused_computation.22.clone.1 | convolution fusion | flops 134348800 | bytes 1703940 | tf_op jit(solution)/shard_map/while/body/eval_jaxpr/hijt,hjtd->hid/dot_general | solution.py:125
  58.7 1.2 %fusion.123 = bf16[3,2,4,256,128]{4,3,2,1,0:T(8,128)(2,1)} fusion(bf16[3,2,4,256,128]{4,3,2,1,0:T(8,128)(2,1)} %get-tuple-element.256, s32[]{:T(128)S(6)} %copy.163, bf16[2,256,4,256]{1,3,2,0:T(8,128)(2,1)S(1)} %multiply_convert_fusion.2, bf16[6,256,128]{2,1,0:T(8,128)(2,1)S(1)} %get-tuple-element.276, s32[]{:T(128)S(6)} %select_n.52), kind=kOutput, calls=%fused_computation.13.clone.1 | convolution fusion | flops 134742016 | bytes 1703944 | tf_op jit(solution)/shard_map/while/body/eval_jaxpr/hijt,hid->hjtd/dot_general | solution.py:129
  59.9 1.2 %dynamic_slice.82 = s32[1]{0:T(128)} dynamic-slice(s32[3]{0:T(128)} %get-tuple-element.274, s32[]{:T(128)S(6)} %copy.163), dynamic_slice_sizes={1} | dynamic-slice | bytes 12 | tf_op jit(solution)/shard_map/while/body/jit(dynamic_index_in_dim)/dynamic_slice | solution.py:139
  61.7 0.6 constant_dynamic-slice_fusion.11
  62.3 0.7 copy.153
  63.0 0.8 constant_dynamic-slice_fusion.10
  63.8 0.7 convolution_convert_fusion.13
  64.5 0.7 convolution_convert_fusion.14
  65.7 0.5 fusion.120
  66.2 1.5 %fusion.121 = bf16[3,2,256,128]{3,2,1,0:T(8,128)(2,1)} fusion(bf16[3,2,256,128]{3,2,1,0:T(8,128)(2,1)} %get-tuple-element.254, s32[]{:T(128)S(6)} %copy.163, bf16[2,4,256,128]{3,1,2,0:T(4,128)(2,1)S(1)} %convolution_convert_fusion.13, f32[2,256,4,256]{1,3,2,0:T(8,128)S(1)} %get-tuple-element.233, f32[2,256]{1,0:T(2,128)S(1)} %fusion.120, ...), kind=kOutput, calls=%fused_computation.24.clone.1 | convolution fusion | flops 136904704 | bytes 2756620 | tf_op jit(solution)/shard_map/while/body/eval_jaxpr/hijt,hjtd->hid/dot_general | solution.py:116
  67.7 1.5 %fusion.124 = bf16[3,2,4,256,128]{4,3,2,1,0:T(8,128)(2,1)} fusion(bf16[3,2,4,256,128]{4,3,2,1,0:T(8,128)(2,1)} %get-tuple-element.257, s32[]{:T(128)S(6)} %copy.163, bf16[6,256,128]{2,1,0:T(8,128)(2,1)S(1)} %copy-done.19, s32[]{:T(128)S(6)} %select_n.52, f32[2,256,4,256]{1,3,2,0:T(8,128)S(1)} %get-tuple-element.233, f32[2,256]{1,0:T(2,128)S(1)} %fusion.120, ...), kind=kOutput, calls=%fused_computation.15.clone.1 | convolution fusion | flops 137101312 | bytes 2757128 | tf_op jit(solution)/shard_map/while/body/eval_jaxpr/hijt,hid->hjtd/dot_general | solution.py:134
  69.2 0.8 multiply_reduce_fusion.2
  69.9 0.8 multiply_convert_fusion.2
  70.7 1.2 %fusion.122 = bf16[3,2,256,128]{3,2,1,0:T(8,128)(2,1)} fusion(bf16[3,2,256,128]{3,2,1,0:T(8,128)(2,1)} %get-tuple-element.255, s32[]{:T(128)S(6)} %copy.163, bf16[2,256,4,256]{1,3,2,0:T(8,128)(2,1)S(1)} %multiply_convert_fusion.2, bf16[2,4,256,128]{3,1,2,0:T(4,128)(2,1)S(1)} %convolution_convert_fusion.14), kind=kOutput, calls=%fused_computation.22.clone.1 | convolution fusion | flops 134348800 | bytes 1703940 | tf_op jit(solution)/shard_map/while/body/eval_jaxpr/hijt,hjtd->hid/dot_general | solution.py:125
  71.9 1.2 %fusion.123 = bf16[3,2,4,256,128]{4,3,2,1,0:T(8,128)(2,1)} fusion(bf16[3,2,4,256,128]{4,3,2,1,0:T(8,128)(2,1)} %get-tuple-element.256, s32[]{:T(128)S(6)} %copy.163, bf16[2,256,4,256]{1,3,2,0:T(8,128)(2,1)S(1)} %multiply_convert_fusion.2, bf16[6,256,128]{2,1,0:T(8,128)(2,1)S(1)} %get-tuple-element.276, s32[]{:T(128)S(6)} %select_n.52), kind=kOutput, calls=%fused_computation.13.clone.1 | convolution fusion | flops 134742016 | bytes 1703944 | tf_op jit(solution)/shard_map/while/body/eval_jaxpr/hijt,hid->hjtd/dot_general | solution.py:129
  73.2 2.8 %fusion.49 = bf16[3,1,6,256,128]{4,0,3,2,1:T(4,128)(2,1)S(1)} fusion(bf16[6,4,256,128]{3,2,1,0:T(8,128)(2,1)} %bitcast.218, pred[6,4,3]{1,2,0:T(4,128)(4,1)} %get-tuple-element.134), kind=kOutput, calls=%fused_computation.73 | convolution fusion | flops 5308416 | bytes 2752584 | tf_op jit(solution)/shard_map/hjc,hjtd->chtd/dot_general | solution.py:147
  76.1 1.3 %fusion.46 = bf16[3,1,6,256,128]{4,0,3,2,1:T(4,128)(2,1)S(1)} fusion(bf16[6,4,256,128]{3,2,1,0:T(8,128)(2,1)S(1)} %bitcast.219, pred[6,4,3]{1,2,0:T(4,128)(4,1)S(1)} %copy-done.4), kind=kOutput, calls=%fused_computation.72 | convolution fusion | flops 5308416 | bytes 2752584 | tf_op jit(solution)/shard_map/hjc,hjtd->chtd/dot_general | solution.py:144
  77.4 4.0 %pad_maximum_fusion.1 = (bf16[1,2,6,256,128]{4,0,3,2,1:T(2,128)(2,1)S(1)}, f32[1,2,6,256,128]{4,0,3,2,1:T(1,128)S(1)}, bf16[1,2,6,256,128]{4,0,3,2,1:T(2,128)(2,1)S(1)}) fusion(bf16[3,1,6,256,128]{4,0,3,2,1:T(4,128)(2,1)S(1)} %fusion.49, bf16[3,1,6,256,128]{4,0,3,2,1:T(4,128)(2,1)S(1)} %fusion.46), kind=kLoop, calls=%fused_computation.61 | loop fusion | flops 4718592 | bytes 5505024 | tf_op jit(solution)/shard_map/stack | solution.py:150
  81.4 1.0 fusion.56
  82.4 3.8 %collective-permute-start.2 = (bf16[2,3,256,128]{3,1,2,0:T(4,128)(2,1)S(1)}, bf16[2,3,256,128]{3,1,2,0:T(4,128)(2,1)S(1)}, u32[]{:S(2)}, u32[]{:S(2)}) collective-permute-start(bf16[2,3,256,128]{3,1,2,0:T(4,128)(2,1)S(1)} %fusion.56), channel_id=1, source_target_pairs={{0,2},{2,4},{4,6},{6,8},{8,10},{10,12},{12,14},{1,3},{3,5},{5,7},{... | collective-permute-start | bytes 1179656 | tf_op jit(solution)/shard_map/ppermute | solution.py:13
  86.3 1.0 fusion.57
  87.3 2.0 %collective-permute-start.3 = (bf16[2,3,256,128]{3,1,2,0:T(4,128)(2,1)S(1)}, bf16[2,3,256,128]{3,1,2,0:T(4,128)(2,1)S(1)}, u32[]{:S(2)}, u32[]{:S(2)}) collective-permute-start(bf16[2,3,256,128]{3,1,2,0:T(4,128)(2,1)S(1)} %fusion.57), channel_id=1, source_target_pairs={{2,0},{4,2},{6,4},{8,6},{10,8},{12,10},{14,12},{3,1},{5,3},{7,5},{... | collective-permute-start | bytes 1179656 | tf_op jit(solution)/shard_map/ppermute | solution.py:13
  89.3 19.3 %collective-permute-done.2 = bf16[2,3,256,128]{3,1,2,0:T(4,128)(2,1)S(1)} collective-permute-done((bf16[2,3,256,128]{3,1,2,0:T(4,128)(2,1)S(1)}, bf16[2,3,256,128]{3,1,2,0:T(4,128)(2,1)S(1)}, u32[]{:S(2)}, u32[]{:S(2)}) %collective-permute-start.2) | collective-permute-done | bytes 393248 | tf_op jit(solution)/shard_map/ppermute | solution.py:13
  108.6 0.5 fusion.83
  109.1 0.5 fusion.78
  109.8 0.9 slice_bitcast_fusion
  (86 shorter events, 3.9 us)
Async XLA Ops:
  1.9 1.9 %copy-start.9 = (pred[6]{0:T(512)(128)(4,1)}, pred[6]{0:T(512)(128)(4,1)S(1)}, u32[]{:S(2)}) copy-start(pred[6]{0:T(512)(128)(4,1)S(1)} %get-tuple-element.132) | copy-start | bytes 22
  2.1 5.6 %copy-start.13 = (s32[6]{0:T(128)}, s32[6]{0:T(128)S(1)}, u32[]{:S(2)}) copy-start(s32[6]{0:T(128)S(1)} %add_bitcast_fusion.1) | copy-start | bytes 76
  4.2 26.8 %collective-permute-start.1 = (bf16[2,3,256,128]{3,1,2,0:T(4,128)(2,1)S(1)}, bf16[2,3,256,128]{3,1,2,0:T(4,128)(2,1)S(1)}, u32[]{:S(2)}, u32[]{:S(2)}) collective-permute-start(bf16[2,3,256,128]{3,1,2,0:T(4,128)(2,1)S(1)} %fusion.55), channel_id=1, source_target_pairs={{0,2},{2,4},{4,6},{6,8},{8,10},{10,12},{12,14},{1,3},{3,5},{5,7},{... | collective-permute-start | bytes 1179656 | tf_op jit(solution)/shard_map/ppermute | solution.py:13
  7.7 0.5 copy-start.11
  7.9 0.6 copy-start.15
  8.9 22.6 %collective-permute-start = (bf16[2,3,256,128]{3,1,2,0:T(4,128)(2,1)S(1)}, bf16[2,3,256,128]{3,1,2,0:T(4,128)(2,1)S(1)}, u32[]{:S(2)}, u32[]{:S(2)}) collective-permute-start(bf16[2,3,256,128]{3,1,2,0:T(4,128)(2,1)S(1)} %fusion.54), channel_id=1, source_target_pairs={{2,0},{4,2},{6,4},{8,6},{10,8},{12,10},{14,12},{3,1},{5,3},{7,5},{... | collective-permute-start | bytes 1179656 | tf_op jit(solution)/shard_map/ppermute | solution.py:13
  11.7 19.8 %copy-start.5 = (s32[6]{0:T(128)}, s32[6]{0:T(128)S(1)}, u32[]{:S(2)}) copy-start(s32[6]{0:T(128)S(1)} %add_bitcast_fusion.2) | copy-start | bytes 76
  11.7 19.8 %copy-start.2 = (pred[6]{0:T(512)(128)(4,1)}, pred[6]{0:T(512)(128)(4,1)S(1)}, u32[]{:S(2)}) copy-start(pred[6]{0:T(512)(128)(4,1)S(1)} %get-tuple-element.130) | copy-start | bytes 22
  14.2 17.8 %copy-start = (bf16[1,2,6,256,128]{4,2,3,1,0:T(8,128)(2,1)S(1)}, bf16[1,2,6,256,128]{4,2,3,1,0:T(8,128)(2,1)}, u32[]{:S(2)}) copy-start(bf16[1,2,6,256,128]{4,2,3,1,0:T(8,128)(2,1)} %fusion.62) | copy-start | bytes 2359300
  14.2 17.3 %copy-start.7 = (s32[6]{0:T(128)}, s32[6]{0:T(128)S(1)}, u32[]{:S(2)}) copy-start(s32[6]{0:T(128)S(1)} %add_bitcast_fusion) | copy-start | bytes 76
  32.0 1.3 %copy-start.1 = (bf16[6,256,128]{2,1,0:T(8,128)(2,1)S(1)}, bf16[6,256,128]{2,1,0:T(8,128)(2,1)}, u32[]{:S(2)}) copy-start(bf16[6,256,128]{2,1,0:T(8,128)(2,1)} %param.7) | copy-start | bytes 1179652
  33.4 1.8 %copy-start.17 = (pred[6,4]{0,1:T(4,128)(4,1)}, pred[6,4]{0,1:T(4,128)(4,1)S(1)}, u32[]{:S(2)}) copy-start(pred[6,4]{0,1:T(4,128)(4,1)S(1)} %get-tuple-element.275) | copy-start | bytes 76 | tf_op jit(solution)/shard_map/while
  39.6 1.5 %copy-start.19 = (bf16[6,256,128]{2,1,0:T(8,128)(2,1)S(1)}, bf16[6,256,128]{2,1,0:T(8,128)(2,1)}, u32[]{:S(2)}) copy-start(bf16[6,256,128]{2,1,0:T(8,128)(2,1)} %get-tuple-element.279) | copy-start | bytes 1179652 | tf_op jit(solution)/shard_map/while
  44.2 2.5 %copy-start.18 = (pred[6,4]{0,1:T(4,128)(4,1)S(1)}, pred[6,4]{0,1:T(4,128)(4,1)}, u32[]{:S(2)}) copy-start(pred[6,4]{0,1:T(4,128)(4,1)} %copy-done.17) | copy-start | bytes 76 | tf_op jit(solution)/shard_map/while
  46.6 1.8 %copy-start.17 = (pred[6,4]{0,1:T(4,128)(4,1)}, pred[6,4]{0,1:T(4,128)(4,1)S(1)}, u32[]{:S(2)}) copy-start(pred[6,4]{0,1:T(4,128)(4,1)S(1)} %get-tuple-element.275) | copy-start | bytes 76 | tf_op jit(solution)/shard_map/while
  52.9 1.5 %copy-start.19 = (bf16[6,256,128]{2,1,0:T(8,128)(2,1)S(1)}, bf16[6,256,128]{2,1,0:T(8,128)(2,1)}, u32[]{:S(2)}) copy-start(bf16[6,256,128]{2,1,0:T(8,128)(2,1)} %get-tuple-element.279) | copy-start | bytes 1179652 | tf_op jit(solution)/shard_map/while
  57.4 2.5 %copy-start.18 = (pred[6,4]{0,1:T(4,128)(4,1)S(1)}, pred[6,4]{0,1:T(4,128)(4,1)}, u32[]{:S(2)}) copy-start(pred[6,4]{0,1:T(4,128)(4,1)} %copy-done.17) | copy-start | bytes 76 | tf_op jit(solution)/shard_map/while
  59.9 1.8 %copy-start.17 = (pred[6,4]{0,1:T(4,128)(4,1)}, pred[6,4]{0,1:T(4,128)(4,1)S(1)}, u32[]{:S(2)}) copy-start(pred[6,4]{0,1:T(4,128)(4,1)S(1)} %get-tuple-element.275) | copy-start | bytes 76 | tf_op jit(solution)/shard_map/while
  66.2 1.5 %copy-start.19 = (bf16[6,256,128]{2,1,0:T(8,128)(2,1)S(1)}, bf16[6,256,128]{2,1,0:T(8,128)(2,1)}, u32[]{:S(2)}) copy-start(bf16[6,256,128]{2,1,0:T(8,128)(2,1)} %get-tuple-element.279) | copy-start | bytes 1179652 | tf_op jit(solution)/shard_map/while
  70.7 2.5 %copy-start.18 = (pred[6,4]{0,1:T(4,128)(4,1)S(1)}, pred[6,4]{0,1:T(4,128)(4,1)}, u32[]{:S(2)}) copy-start(pred[6,4]{0,1:T(4,128)(4,1)} %copy-done.17) | copy-start | bytes 76 | tf_op jit(solution)/shard_map/while
  73.2 2.8 %copy-start.4 = (pred[6,4,3]{1,2,0:T(4,128)(4,1)S(1)}, pred[6,4,3]{1,2,0:T(4,128)(4,1)}, u32[]{:S(2)}) copy-start(pred[6,4,3]{1,2,0:T(4,128)(4,1)} %get-tuple-element.134) | copy-start | bytes 220
  73.2 2.9 %copy-start.20 = (bf16[3,2,4,256,128]{4,3,2,1,0:T(8,128)(2,1)S(1)}, bf16[3,2,4,256,128]{4,3,2,1,0:T(8,128)(2,1)}, u32[]{:S(2)}) copy-start(bf16[3,2,4,256,128]{4,3,2,1,0:T(8,128)(2,1)} %get-tuple-element.66) | copy-start | bytes 4718596
  77.4 4.0 %copy-start.6 = (s32[6]{0:T(128)S(1)}, s32[6]{0:T(128)}, u32[]{:S(2)}) copy-start(s32[6]{0:T(128)} %copy-done.5) | copy-start | bytes 76
  77.4 8.9 %copy-start.3 = (pred[6]{0:T(512)(128)(4,1)S(1)}, pred[6]{0:T(512)(128)(4,1)}, u32[]{:S(2)}) copy-start(pred[6]{0:T(512)(128)(4,1)} %copy-done.2) | copy-start | bytes 22
  77.4 8.9 %copy-start.8 = (s32[6]{0:T(128)S(1)}, s32[6]{0:T(128)}, u32[]{:S(2)}) copy-start(s32[6]{0:T(128)} %copy-done.7) | copy-start | bytes 76
  81.4 27.2 %copy-start.12 = (pred[6]{0:T(512)(128)(4,1)S(1)}, pred[6]{0:T(512)(128)(4,1)}, u32[]{:S(2)}) copy-start(pred[6]{0:T(512)(128)(4,1)} %copy-done.11) | copy-start | bytes 22
  81.4 27.2 %copy-start.16 = (s32[6]{0:T(128)S(1)}, s32[6]{0:T(128)}, u32[]{:S(2)}) copy-start(s32[6]{0:T(128)} %copy-done.15) | copy-start | bytes 76
  81.4 27.7 %copy-start.10 = (pred[6]{0:T(512)(128)(4,1)S(1)}, pred[6]{0:T(512)(128)(4,1)}, u32[]{:S(2)}) copy-start(pred[6]{0:T(512)(128)(4,1)} %copy-done.9) | copy-start | bytes 22
  81.4 27.7 %copy-start.14 = (s32[6]{0:T(128)S(1)}, s32[6]{0:T(128)}, u32[]{:S(2)}) copy-start(s32[6]{0:T(128)} %copy-done.13) | copy-start | bytes 76
  82.4 26.1 %collective-permute-start.2 = (bf16[2,3,256,128]{3,1,2,0:T(4,128)(2,1)S(1)}, bf16[2,3,256,128]{3,1,2,0:T(4,128)(2,1)S(1)}, u32[]{:S(2)}, u32[]{:S(2)}) collective-permute-start(bf16[2,3,256,128]{3,1,2,0:T(4,128)(2,1)S(1)} %fusion.56), channel_id=1, source_target_pairs={{0,2},{2,4},{4,6},{6,8},{8,10},{10,12},{12,14},{1,3},{3,5},{5,7},{... | collective-permute-start | bytes 1179656 | tf_op jit(solution)/shard_map/ppermute | solution.py:13
  87.3 21.8 %collective-permute-start.3 = (bf16[2,3,256,128]{3,1,2,0:T(4,128)(2,1)S(1)}, bf16[2,3,256,128]{3,1,2,0:T(4,128)(2,1)S(1)}, u32[]{:S(2)}, u32[]{:S(2)}) collective-permute-start(bf16[2,3,256,128]{3,1,2,0:T(4,128)(2,1)S(1)} %fusion.57), channel_id=1, source_target_pairs={{2,0},{4,2},{6,4},{8,6},{10,8},{12,10},{14,12},{3,1},{5,3},{7,5},{... | collective-permute-start | bytes 1179656 | tf_op jit(solution)/shard_map/ppermute | solution.py:13
where the time goes:
time: 113 us; the launch traced here: 111 us
  waiting for transfers between devices  36.1 us (32%)
  matrix products  33.3 us (29%)
  local copies, waits for them, and re-layouts  15.4 us (14%)
  starting transfers between devices  11.7 us (10%)
  other arithmetic  11.4 us (10%)
  loops' own time  1.87 us (2%)
    ppermute x4, waiting for transfers between devices, passed_along(): return lax.ppermute(block, axis, route)  36.1 us
    ppermute x4, starting transfers between devices, passed_along(): return lax.ppermute(block, axis, route)  11.7 us
    dot_general x3, matrix products, attend(): jnp.einsum('hijt,hjtd->hid', probs_low, value_chosen, preferred_element_t...  4.53 us
    dot_general x3, matrix products, attend(): jnp.einsum('hijt,hid->hjtd', probs_low, grad_block, preferred_element_typ...  4.39 us
    another operation x1, other arithmetic, per_device(): returned_terms = jnp.stack([key_back, value_back], axis=1)  3.95 us
    dynamic_slice x6, local copies, waits for them, and re-layouts, attend(): live_block = lax.dynamic_slice_in_dim(live_slots, first_head, 2, 0)  3.83 us
    dot_general x3, matrix products, attend(): jnp.einsum('hijt,hid->hjtd', score_grad, query_block, preferred_element_t...  3.72 us
    dot_general x3, matrix products, attend(): jnp.einsum('hijt,hjtd->hid', score_grad, key_chosen, preferred_element_ty...  3.66 us
  transfers between devices with their start and end apart: 4, of which 2 were waited for; matrix products, arithmetic and copies ran while one was open for 5% of the time, Pallas kernels for 0%

commit v1 on v0

v1 whole, which is shorter than its diff:
```python
import functools

import jax
import jax.numpy as jnp
from jax import lax
from jax.experimental import pallas as pl
from jax.experimental.pallas import tpu as pltpu
from jax.sharding import PartitionSpec as P

HCAP = 3
GX = 8
MASKED = -1e30


def directions(tile_count):
    row_tiles = min(4, tile_count // GX)
    layer_size = GX * row_tiles
    layers = tile_count // layer_size
    result = []
    for stride, extent in ((1, GX), (GX, row_tiles), (layer_size, layers)):
        if extent > 1:
            result += [(stride, extent, 1), (stride, extent, -1)]
    return result


def dot_rows(a, b):
    return lax.dot_general(a, b, (((1,), (1,)), ((), ())), preferred_element_type=jnp.float32)


def dot_plain(a, b):
    return lax.dot_general(a, b, (((1,), (0,)), ((), ())), preferred_element_type=jnp.float32)


def dot_first(a, b):
    return lax.dot_general(a, b, (((0,), (0,)), ((), ())), preferred_element_type=jnp.float32)


def kernel(
    dims,
    lists,
    q,
    k,
    v,
    g,
    out,
    qg,
    kg,
    vg,
    k_pack,
    v_pack,
    k_in,
    v_in,
    kp_pack,
    vp_pack,
    kp_in,
    vp_in,
    p32,
    p16,
    s16,
    kg32,
    vg32,
    read_slot,
    owed_slot,
    f_send,
    f_recv,
    b_send,
    b_recv,
):
    tile_count, entries, cap = dims
    heads, rows, width = q.shape
    scale = width ** (-0.5)
    dirs = directions(tile_count)
    nd = len(dirs)
    E = nd + 1
    none = nd * cap
    me = lax.axis_index("seq")

    inside, beside = [], []
    for stride, extent, sign in dirs:
        at = (me // stride) % extent + sign
        ok = (at >= 0) & (at < extent)
        inside.append(ok)
        beside.append(jnp.where(ok, me + sign * stride, me))

    barrier = pltpu.get_barrier_semaphore()
    for d in range(nd):

        @pl.when(inside[d])
        def _(d=d):
            pl.semaphore_signal(
                barrier,
                inc=1,
                device_id={"seq": beside[d]},
                device_id_type=pl.DeviceIdType.MESH,
            )

    def table(reader, named, ok, slot_ref, d):
        count = jnp.int32(0)
        held = [jnp.int32(0)] * cap
        for h in range(heads):
            hit = jnp.int32(0)
            for j in range(1, entries):
                entry = lists[(h * tile_count + reader) * entries + j]
                hit = hit | (entry == named).astype(jnp.int32)
            hit = hit * ok.astype(jnp.int32)
            slot_ref[d * heads + h] = jnp.where(
                hit == 1, d * cap + jnp.minimum(count, cap - 1), none
            )
            held = [
                jnp.where((hit == 1) & (count == s), jnp.int32(h), held[s]) for s in range(cap)
            ]
            count = count + hit
        return held

    owed_head = [table(beside[d], me, inside[d], owed_slot, d) for d in range(nd)]
    for d in range(nd):
        for s in range(cap):
            k_pack[d * cap + s] = k[owed_head[d][s]]
    for d in range(nd):
        for s in range(cap):
            v_pack[d * cap + s] = v[owed_head[d][s]]

    pl.semaphore_wait(barrier, sum(ok.astype(jnp.int32) for ok in inside))

    def forward(kind, d, to):
        src, dst = ((k_pack, k_in), (v_pack, v_in))[kind]
        return pltpu.make_async_remote_copy(
            src_ref=src.at[pl.ds(d * cap, cap)],
            dst_ref=dst.at[pl.ds(to * cap, cap)],
            send_sem=f_send.at[kind, d],
            recv_sem=f_recv.at[kind, to],
            device_id={"seq": beside[d]},
            device_id_type=pl.DeviceIdType.MESH,
        )

    def backward(kind, d, s, to):
        src, dst = ((vp_pack, vp_in), (kp_pack, kp_in))[kind]
        return pltpu.make_async_remote_copy(
            src_ref=src.at[d * cap + s],
            dst_ref=dst.at[to * cap + s],
            send_sem=b_send.at[kind, d * cap + s],
            recv_sem=b_recv.at[kind, to * cap + s],
            device_id={"seq": beside[d]},
            device_id_type=pl.DeviceIdType.MESH,
        )

    for kind in range(2):
        for d in range(nd):

            @pl.when(inside[d])
            def _(kind=kind, d=d):
                forward(kind, d, d ^ 1).start()

    read_head = [table(me, beside[d], inside[d], read_slot, d) for d in range(nd)]
    blank = jnp.zeros((rows, width), q.dtype)
    k_in[none] = blank
    v_in[none] = blank
    kp_in[none] = blank
    vp_in[none] = blank

    def own_scores(h, carry):
        p32[h * E] = dot_rows(k[h], q[h]) * scale
        return carry

    lax.fori_loop(0, heads, own_scores, 0)

    def arrived(kind):
        for d in range(nd):

            @pl.when(inside[d])
            def _(d=d):
                forward(kind, d, d).wait_recv()

    arrived(0)

    def softmax(h, carry):
        scores = [p32[h * E]]
        for d in range(nd):
            slot = read_slot[d * heads + h]
            bias = jnp.where(slot == none, jnp.float32(MASKED), jnp.float32(0.0))
            scores.append(dot_rows(k_in[slot], q[h]) * scale + bias)
        top = functools.reduce(
            jnp.maximum, [jnp.max(s, axis=0, keepdims=True) for s in scores]
        )
        weights = [jnp.exp(s - top) for s in scores]
        total = sum(jnp.sum(w, axis=0, keepdims=True) for w in weights)
        inverse = 1.0 / total
        for e in range(E):
            prob = weights[e] * inverse
            p32[h * E + e] = prob
            p16[h * E + e] = prob.astype(p16.dtype)
        return carry

    lax.fori_loop(0, heads, softmax, 0)

    for d in range(nd):
        for s in range(cap):
            h = read_head[d][s]
            part = dot_plain(p16[h * E + d + 1], g[h])
            vp_pack[d * cap + s] = part.astype(vp_pack.dtype)
        for s in range(cap):

            @pl.when(inside[d])
            def _(d=d, s=s):
                backward(0, d, s, d ^ 1).start()

    arrived(1)

    def score_grads(h, carry):
        blocks = [v[h]] + [v_in[read_slot[d * heads + h]] for d in range(nd)]
        grads = [dot_rows(block, g[h]) for block in blocks]
        delta = sum(
            jnp.sum(p32[h * E + e] * grads[e], axis=0, keepdims=True) for e in range(E)
        )
        for e in range(E):
            s16[h * E + e] = (p32[h * E + e] * (grads[e] - delta)).astype(s16.dtype)
        return carry

    lax.fori_loop(0, heads, score_grads, 0)

    for d in range(nd):
        for s in range(cap):
            h = read_head[d][s]
            part = dot_plain(s16[h * E + d + 1], q[h]) * scale
            kp_pack[d * cap + s] = part.astype(kp_pack.dtype)
        for s in range(cap):

            @pl.when(inside[d])
            def _(d=d, s=s):
                backward(1, d, s, d ^ 1).start()

    def own_results(h, carry):
        slots = [read_slot[d * heads + h] for d in range(nd)]
        attn = dot_first(p16[h * E], v[h])
        grad = dot_first(s16[h * E], k[h])
        for d in range(nd):
            attn += dot_first(p16[h * E + d + 1], v_in[slots[d]])
            grad += dot_first(s16[h * E + d + 1], k_in[slots[d]])
        out[h] = attn.astype(out.dtype)
        qg[h] = (grad * scale).astype(qg.dtype)
        kg32[h] = dot_plain(s16[h * E], q[h]) * scale
        vg32[h] = dot_plain(p16[h * E], g[h])
        return carry

    lax.fori_loop(0, heads, own_results, 0)

    for kind, total, terms, result in ((0, vg32, vp_in, vg), (1, kg32, kp_in, kg)):
        for d in range(nd):

            @pl.when(inside[d])
            def _(kind=kind, d=d):
                for s in range(cap):
                    backward(kind, d, s, d).wait_recv()

        def add_terms(h, carry, total=total, terms=terms, result=result):
            value = total[h]
            for d in range(nd):
                value += terms[owed_slot[d * heads + h]].astype(jnp.float32)
            result[h] = value.astype(result.dtype)
            return carry

        lax.fori_loop(0, heads, add_terms, 0)

    for kind in range(2):
        for d in range(nd):

            @pl.when(inside[d])
            def _(kind=kind, d=d):
                forward(kind, d, d ^ 1).wait_send()
                for s in range(cap):
                    backward(kind, d, s, d ^ 1).wait_send()


def per_device(queries, keys, values, out_grad, tile_lists):
    heads, rows, width = queries.shape
    tile_count = lax.axis_size("seq")
    entries = tile_lists.shape[2]
    cap = HCAP * max(1, heads // 6)
    nd = len(directions(tile_count))
    E = nd + 1
    low = queries.dtype
    shape = jax.ShapeDtypeStruct(queries.shape, low)
    vmem = pl.BlockSpec(memory_space=pltpu.VMEM)
    packed = pltpu.VMEM((nd * cap, rows, width), low)
    landed = pltpu.VMEM((nd * cap + 1, rows, width), low)
    wide = pltpu.VMEM((heads, rows, width), jnp.float32)
    return pl.pallas_call(
        functools.partial(kernel, (tile_count, entries, cap)),
        out_shape=(shape,) * 4,
        in_specs=[pl.BlockSpec(memory_space=pltpu.SMEM)] + [vmem] * 4,
        out_specs=(vmem,) * 4,
        scratch_shapes=[
            packed,
            packed,
            landed,
            landed,
            packed,
            packed,
            landed,
            landed,
            pltpu.VMEM((heads * E, rows, rows), jnp.float32),
            pltpu.VMEM((heads * E, rows, rows), low),
            pltpu.VMEM((heads * E, rows, rows), low),
            wide,
            wide,
            pltpu.SMEM((nd * heads,), jnp.int32),
            pltpu.SMEM((nd * heads,), jnp.int32),
            pltpu.SemaphoreType.DMA((2, nd)),
            pltpu.SemaphoreType.DMA((2, nd)),
            pltpu.SemaphoreType.DMA((2, nd * cap)),
            pltpu.SemaphoreType.DMA((2, nd * cap)),
        ],
        compiler_params=pltpu.CompilerParams(
            collective_id=0, has_side_effects=True, vmem_limit_bytes=60 * 1024 * 1024
        ),
        name="tile_attention",
    )(tile_lists.reshape(-1), queries, keys, values, out_grad)


def solution(mesh):
    tokens = P("mp", ("clips", "seq"), None)
    return jax.shard_map(
        per_device,
        mesh=mesh,
        in_specs=(tokens, tokens, tokens, tokens, P("mp", None, None)),
        out_specs=(tokens,) * 4,
        check_vma=False,
    )
```

time: 113 us -> 47.9 us (0.42); the launches traced: 111 us -> 47.6 us
  Pallas kernels: 0 us -> 40.6 us
  waiting for transfers between devices: 36.1 us -> 0 us
  matrix products: 33.3 us -> 0 us
  starting transfers between devices: 11.7 us -> 0 us
  other arithmetic: 11.4 us -> 0 us
  local copies, waits for them, and re-layouts: 15.4 us -> 6.32 us
  loops' own time: 1.87 us -> 0 us
    pallas_call x0 -> x1, Pallas kernels: none -> 40.6 us  [per_device(): pl.pallas_call(functools.partial(kernel, (tile_count, entries, cap)), out...]
    ppermute x4 -> x0, waiting for transfers between devices: 36.1 us -> none  [passed_along(): return lax.ppermute(block, axis, route)]
    dot_general x34 -> x0, matrix products: 33.3 us -> none  [the longest x3 4.53 us: attend(): jnp.einsum('hijt,hjtd->hid', probs_low, value_chosen, preferred_element_t...]
    ppermute x4 -> x0, starting transfers between devices: 11.7 us -> none  [passed_along(): return lax.ppermute(block, axis, route)]
    dynamic_slice x10 -> x0, local copies, waits for them, and re-layouts: 8.37 us -> none  [the longest x6 3.83 us: attend(): live_block = lax.dynamic_slice_in_dim(live_slots, first_head, 2, 0)]
    another operation x12 -> x0, other arithmetic: 6.87 us -> none  [the longest x1 3.95 us: per_device(): returned_terms = jnp.stack([key_back, value_back], axis=1)]
    unnamed x40 -> x11, local copies, waits for them, and re-layouts: 1.08 us -> 5.65 us
    convert_element_type x8 -> x0, other arithmetic: 2.99 us -> none  [the longest x3 2.35 us: attend(): score_grad = (probs * (prob_grad - delta)).astype(jnp.bfloat16)]
  transfers between devices with their start and end apart: 4 -> 0, of which waited for: 2 -> 0; matrix products, arithmetic and copies ran while one was open for 5% -> 0% of each run, Pallas kernels for 0% -> 0%
where the time goes in v1:
time: 47.9 us; the launch traced here: 47.6 us
  Pallas kernels  40.6 us (85%)
  local copies, waits for them, and re-layouts  6.32 us (13%)
  between operations  0.65 us (1%)
    pallas_call x1, Pallas kernels, per_device(): pl.pallas_call(functools.partial(kernel, (tile_count, entries, cap)), out...  40.6 us
    unnamed x11, local copies, waits for them, and re-layouts  5.65 us

profile of v1, /device:TPU:18, one launch (start us, length us, event | category | flops | bytes accessed | tf_op | source)
XLA Modules:
  0.0 47.6 jit_solution(5430129220568914030)
XLA Ops:
  0.6 0.8 %copy.9 = s32[6,8,4]{2,1,0:T(8,128)S(1)} copy(s32[6,8,4]{1,2,0:T(4,128)} %param.9) | data formatting | bytes 1536 | tf_op args[4]
  1.4 0.7 %reshape.11.lists = s32[192]{0:T(256)} reshape(s32[6,8,4]{2,1,0:T(8,128)S(1)} %copy.9) | data formatting | bytes 1536 | tf_op jit(solution)/shard_map/reshape | solution.py:317
  2.1 40.6 %tile_attention.1 = (bf16[6,256,128]{2,1,0:T(8,128)(2,1)}, bf16[6,256,128]{2,1,0:T(8,128)(2,1)}, bf16[6,256,128]{2,1,0:T(8,128)(2,1)}, bf16[6,256,128]{2,1,0:T(8,128)(2,1)}) custom-call(s32[192]{0:T(256)} %reshape.11.lists, bf16[6,256,128]{2,1,0:T(8,128)(2,1)} %q.1, bf16[6,256,128]{2,1,0:T(8,128)(2,1)} %k.1, bf16[6,256,128]{2,1,0:T(8,128)(2,1)} %v.1, ...), custom_call_target="tpu_custom_call" | custom-call | tf_op jit(solution)/shard_map/tile_attention/pallas_call | solution.py:287
  42.7 0.0 copy-start.2
  42.7 1.8 %copy.14 = bf16[6,256,128]{2,1,0:T(8,128)(2,1)} copy(bf16[6,256,128]{2,1,0:T(8,128)(2,1)} %get-tuple-element.8) | data formatting | bytes 786432
  44.6 0.0 copy-done.2
  44.6 0.0 copy-start.1
  44.6 0.7 %copy.15 = bf16[6,256,128]{2,1,0:T(8,128)(2,1)} copy(bf16[6,256,128]{2,1,0:T(8,128)(2,1)S(1)} %copy-done.2) | data formatting | bytes 786432
  45.3 0.4 copy-done.1
  45.7 0.0 copy-start
  45.7 0.7 %copy.16 = bf16[6,256,128]{2,1,0:T(8,128)(2,1)} copy(bf16[6,256,128]{2,1,0:T(8,128)(2,1)S(1)} %copy-done.1) | data formatting | bytes 786432
  46.5 0.4 copy-done
  46.8 0.7 %copy.17 = bf16[6,256,128]{2,1,0:T(8,128)(2,1)} copy(bf16[6,256,128]{2,1,0:T(8,128)(2,1)S(1)} %copy-done) | data formatting | bytes 786432
Async XLA Ops:
  42.7 1.8 %copy-start.2 = (bf16[6,256,128]{2,1,0:T(8,128)(2,1)S(1)}, bf16[6,256,128]{2,1,0:T(8,128)(2,1)}, u32[]{:S(2)}) copy-start(bf16[6,256,128]{2,1,0:T(8,128)(2,1)} %get-tuple-element.9) | copy-start | bytes 1179652
  44.6 1.1 %copy-start.1 = (bf16[6,256,128]{2,1,0:T(8,128)(2,1)S(1)}, bf16[6,256,128]{2,1,0:T(8,128)(2,1)}, u32[]{:S(2)}) copy-start(bf16[6,256,128]{2,1,0:T(8,128)(2,1)} %get-tuple-element.10) | copy-start | bytes 1179652
  45.7 1.1 %copy-start = (bf16[6,256,128]{2,1,0:T(8,128)(2,1)S(1)}, bf16[6,256,128]{2,1,0:T(8,128)(2,1)}, u32[]{:S(2)}) copy-start(bf16[6,256,128]{2,1,0:T(8,128)(2,1)} %get-tuple-element.11) | copy-start | bytes 1179652

commit v2 on v1

--- a/solution.py
+++ b/solution.py
@@ -38,6 +38,14 @@
 def kernel(
     dims,
     lists,
+    q_hbm,
+    k_hbm,
+    v_hbm,
+    g_hbm,
+    out_hbm,
+    qg_hbm,
+    kg_hbm,
+    vg_hbm,
     q,
     k,
     v,
@@ -65,6 +73,8 @@
     f_recv,
     b_send,
     b_recv,
+    i_sem,
+    o_sem,
 ):
     tile_count, entries, cap = dims
     heads, rows, width = q.shape
@@ -75,6 +85,17 @@
     none = nd * cap
     me = lax.axis_index("seq")
 
+    loads = [
+        pltpu.make_async_copy(src, dst, i_sem.at[n])
+        for n, (src, dst) in enumerate(((k_hbm, k), (v_hbm, v), (q_hbm, q), (g_hbm, g)))
+    ]
+    for load in loads:
+        load.start()
+    stores = [
+        pltpu.make_async_copy(src, dst, o_sem.at[n])
+        for n, (src, dst) in enumerate(((out, out_hbm), (qg, qg_hbm), (vg, vg_hbm), (kg, kg_hbm)))
+    ]
+
     inside, beside = [], []
     for stride, extent, sign in dirs:
         at = (me // stride) % extent + sign
@@ -100,7 +121,7 @@
         for h in range(heads):
             hit = jnp.int32(0)
             for j in range(1, entries):
-                entry = lists[(h * tile_count + reader) * entries + j]
+                entry = lists[h, j, reader]
                 hit = hit | (entry == named).astype(jnp.int32)
             hit = hit * ok.astype(jnp.int32)
             slot_ref[d * heads + h] = jnp.where(
@@ -113,15 +134,6 @@
         return held
 
     owed_head = [table(beside[d], me, inside[d], owed_slot, d) for d in range(nd)]
-    for d in range(nd):
-        for s in range(cap):
-            k_pack[d * cap + s] = k[owed_head[d][s]]
-    for d in range(nd):
-        for s in range(cap):
-            v_pack[d * cap + s] = v[owed_head[d][s]]
-
-    pl.semaphore_wait(barrier, sum(ok.astype(jnp.int32) for ok in inside))
-
     def forward(kind, d, to):
         src, dst = ((k_pack, k_in), (v_pack, v_in))[kind]
         return pltpu.make_async_remote_copy(
@@ -144,7 +156,13 @@
             device_id_type=pl.DeviceIdType.MESH,
         )
 
-    for kind in range(2):
+    for kind, (full, pack) in enumerate(((k, k_pack), (v, v_pack))):
+        loads[kind].wait()
+        for d in range(nd):
+            for s in range(cap):
+                pack[d * cap + s] = full[owed_head[d][s]]
+        if kind == 0:
+            pl.semaphore_wait(barrier, sum(ok.astype(jnp.int32) for ok in inside))
         for d in range(nd):
 
             @pl.when(inside[d])
@@ -157,6 +175,8 @@
     v_in[none] = blank
     kp_in[none] = blank
     vp_in[none] = blank
+    loads[2].wait()
+    loads[3].wait()
 
     def own_scores(h, carry):
         p32[h * E] = dot_rows(k[h], q[h]) * scale
@@ -243,6 +263,8 @@
         return carry
 
     lax.fori_loop(0, heads, own_results, 0)
+    stores[0].start()
+    stores[1].start()
 
     for kind, total, terms, result in ((0, vg32, vp_in, vg), (1, kg32, kp_in, kg)):
         for d in range(nd):
@@ -260,6 +282,7 @@
             return carry
 
         lax.fori_loop(0, heads, add_terms, 0)
+        stores[2 + kind].start()
 
     for kind in range(2):
         for d in range(nd):
@@ -269,6 +292,23 @@
                 forward(kind, d, d ^ 1).wait_send()
                 for s in range(cap):
                     backward(kind, d, s, d ^ 1).wait_send()
+    for store in stores:
+        store.wait()
+
+
+def write_results(*refs):
+    count = (len(refs) - 2) // 3
+    sources, results, held = refs[:count], refs[count : 2 * count], refs[2 * count : 3 * count]
+    in_sem, out_sem = refs[3 * count :]
+    loads = [pltpu.make_async_copy(a, b, in_sem.at[n]) for n, (a, b) in enumerate(zip(sources, held))]
+    stores = [pltpu.make_async_copy(a, b, out_sem.at[n]) for n, (a, b) in enumerate(zip(held, results))]
+    for load in loads:
+        load.start()
+    for load, store in zip(loads, stores):
+        load.wait()
+        store.start()
+    for store in stores:
+        store.wait()
 
 
 def per_device(queries, keys, values, out_grad, tile_lists):
@@ -280,16 +320,18 @@
     E = nd + 1
     low = queries.dtype
     shape = jax.ShapeDtypeStruct(queries.shape, low)
-    vmem = pl.BlockSpec(memory_space=pltpu.VMEM)
+    anywhere = pl.BlockSpec(memory_space=pl.ANY)
+    whole = pltpu.VMEM(queries.shape, low)
     packed = pltpu.VMEM((nd * cap, rows, width), low)
     landed = pltpu.VMEM((nd * cap + 1, rows, width), low)
     wide = pltpu.VMEM((heads, rows, width), jnp.float32)
-    return pl.pallas_call(
+    results = pl.pallas_call(
         functools.partial(kernel, (tile_count, entries, cap)),
         out_shape=(shape,) * 4,
-        in_specs=[pl.BlockSpec(memory_space=pltpu.SMEM)] + [vmem] * 4,
-        out_specs=(vmem,) * 4,
-        scratch_shapes=[
+        in_specs=[pl.BlockSpec(memory_space=pltpu.SMEM)] + [anywhere] * 4,
+        out_specs=(anywhere,) * 4,
+        scratch_shapes=[whole] * 8
+        + [
             packed,
             packed,
             landed,
@@ -309,12 +351,24 @@
             pltpu.SemaphoreType.DMA((2, nd)),
             pltpu.SemaphoreType.DMA((2, nd * cap)),
             pltpu.SemaphoreType.DMA((2, nd * cap)),
+            pltpu.SemaphoreType.DMA((4,)),
+            pltpu.SemaphoreType.DMA((4,)),
         ],
         compiler_params=pltpu.CompilerParams(
             collective_id=0, has_side_effects=True, vmem_limit_bytes=60 * 1024 * 1024
         ),
         name="tile_attention",
-    )(tile_lists.reshape(-1), queries, keys, values, out_grad)
+    )(jnp.swapaxes(tile_lists, 1, 2), queries, keys, values, out_grad)
+    return pl.pallas_call(
+        write_results,
+        out_shape=(shape,) * 4,
+        in_specs=[anywhere] * 4,
+        out_specs=(anywhere,) * 4,
+        scratch_shapes=[whole] * 4
+        + [pltpu.SemaphoreType.DMA((4,)), pltpu.SemaphoreType.DMA((4,))],
+        compiler_params=pltpu.CompilerParams(vmem_limit_bytes=60 * 1024 * 1024),
+        name="write_results",
+    )(*results)
 
 
 def solution(mesh):

time: 47.9 us -> 42.8 us (0.89)
  local copies, waits for them, and re-layouts: 6.32 us -> 0 us
  Pallas kernels: 40.6 us -> 42 us
    unnamed x11 -> x0, local copies, waits for them, and re-layouts: 5.65 us -> none
    pallas_call x0 -> x1, Pallas kernels: none -> 2.2 us  [per_device(): pl.pallas_call(write_results, out_shape=(shape,) * 4, in_specs=[anywhere]...]
    pallas_call x1, Pallas kernels: 40.6 us -> 39.8 us  [per_device(): pl.pallas_call(functools.partial(kernel, (tile_count, entries, cap)), out...]
    reshape x1 -> x0, local copies, waits for them, and re-layouts: 0.67 us -> none  [per_device(): tile_lists.reshape(-1)]
where the time goes in v2:
time: 42.8 us; the launch traced here: 42.6 us
  Pallas kernels  42 us (98%)
  between operations  0.64 us (1%)
    pallas_call x1, Pallas kernels, per_device(): pl.pallas_call(functools.partial(kernel, (tile_count, entries, cap)), out...  39.8 us
    pallas_call x1, Pallas kernels, per_device(): pl.pallas_call(write_results, out_shape=(shape,) * 4, in_specs=[anywhere]...  2.2 us

profile of v2, /device:TPU:18, one launch (start us, length us, event | category | flops | bytes accessed | tf_op | source)
XLA Modules:
  0.0 42.6 jit_solution(14966796289867868135)
XLA Ops:
  0.6 39.8 %tile_attention.1 = (bf16[6,256,128]{2,1,0:T(8,128)(2,1)}, bf16[6,256,128]{2,1,0:T(8,128)(2,1)}, bf16[6,256,128]{2,1,0:T(8,128)(2,1)}, bf16[6,256,128]{2,1,0:T(8,128)(2,1)}) custom-call(s32[6,4,8]{2,1,0:T(4,128)} %bitcast.1, bf16[6,256,128]{2,1,0:T(8,128)(2,1)} %q_hbm.1, bf16[6,256,128]{2,1,0:T(8,128)(2,1)} %k_hbm.1, bf16[6,256,128]{2,1,0:T(8,128)(2,1)} %v_hbm.1, ...), custom_call_target="tpu_custom_call" | custom-call | tf_op jit(solution)/shard_map/tile_attention/pallas_call | solution.py:328
  40.4 2.2 %write_results.1 = (bf16[6,256,128]{2,1,0:T(8,128)(2,1)}, bf16[6,256,128]{2,1,0:T(8,128)(2,1)}, bf16[6,256,128]{2,1,0:T(8,128)(2,1)}, bf16[6,256,128]{2,1,0:T(8,128)(2,1)}) custom-call(bf16[6,256,128]{2,1,0:T(8,128)(2,1)} %get-tuple-element.8.refs_0_, bf16[6,256,128]{2,1,0:T(8,128)(2,1)} %get-tuple-element.9.refs_1_, ...), custom_call_target="tpu_custom_call" | custom-call | tf_op jit(solution)/shard_map/write_results/pallas_call | solution.py:362

commit v3 on v2

--- a/solution.py
+++ b/solution.py
@@ -69,14 +69,15 @@
     vg32,
     read_slot,
     owed_slot,
-    f_send,
-    f_recv,
-    b_send,
-    b_recv,
+    relay_in,
+    send_sem,
+    recv_sem,
+    relay_send,
+    relay_recv,
     i_sem,
     o_sem,
 ):
-    tile_count, entries, cap = dims
+    tile_count, entries, cap, chunks = dims
     heads, rows, width = q.shape
     scale = width ** (-0.5)
     dirs = directions(tile_count)
@@ -103,15 +104,31 @@
         inside.append(ok)
         beside.append(jnp.where(ok, me + sign * stride, me))
 
+    chunk_rows = rows // chunks
+    even, place = me % 2 == 0, me // 2
+    by_relay = [[False] * chunks for _ in range(nd)]
+    hands_on = [[False] * chunks for _ in range(nd)]
+    two_on = []
+    greeted = [(inside[d], beside[d]) for d in range(nd)]
+    if chunks > 1:
+        for d, (_, _, sign) in enumerate(dirs):
+            amount = chunks - 1 - place if sign > 0 else place
+            sends = jnp.logical_not(even) if sign > 0 else even
+            by_relay[d] = [sends & (c < amount) for c in range(chunks)]
+            hands_on[d] = [jnp.logical_not(sends) & (c < amount) for c in range(chunks)]
+            ok = (me + 2 * sign >= 0) & (me + 2 * sign < tile_count)
+            two_on.append(jnp.where(ok, me + 2 * sign, me))
+            greeted.append((ok, two_on[d]))
+
     barrier = pltpu.get_barrier_semaphore()
-    for d in range(nd):
-
-        @pl.when(inside[d])
-        def _(d=d):
+    for ok, other in greeted:
+
+        @pl.when(ok)
+        def _(other=other):
             pl.semaphore_signal(
                 barrier,
                 inc=1,
-                device_id={"seq": beside[d]},
+                device_id={"seq": other},
                 device_id_type=pl.DeviceIdType.MESH,
             )
 
@@ -134,27 +151,85 @@
         return held
 
     owed_head = [table(beside[d], me, inside[d], owed_slot, d) for d in range(nd)]
-    def forward(kind, d, to):
-        src, dst = ((k_pack, k_in), (v_pack, v_in))[kind]
+    packs = (k_pack, v_pack, vp_pack, kp_pack)
+    landings = (k_in, v_in, vp_in, kp_in)
+
+    def piece(ref, d, c):
+        return ref.at[pl.ds(d * cap, cap), pl.ds(c * chunk_rows, chunk_rows)]
+
+    def remote(src, dst, out_sem, in_sem, other):
         return pltpu.make_async_remote_copy(
-            src_ref=src.at[pl.ds(d * cap, cap)],
-            dst_ref=dst.at[pl.ds(to * cap, cap)],
-            send_sem=f_send.at[kind, d],
-            recv_sem=f_recv.at[kind, to],
-            device_id={"seq": beside[d]},
+            src_ref=src,
+            dst_ref=dst,
+            send_sem=out_sem,
+            recv_sem=in_sem,
+            device_id={"seq": other},
             device_id_type=pl.DeviceIdType.MESH,
         )
 
-    def backward(kind, d, s, to):
-        src, dst = ((vp_pack, vp_in), (kp_pack, kp_in))[kind]
-        return pltpu.make_async_remote_copy(
-            src_ref=src.at[d * cap + s],
-            dst_ref=dst.at[to * cap + s],
-            send_sem=b_send.at[kind, d * cap + s],
-            recv_sem=b_recv.at[kind, to * cap + s],
-            device_id={"seq": beside[d]},
-            device_id_type=pl.DeviceIdType.MESH,
-        )
+    def direct(kind, d, c, to):
+        return remote(
+            piece(packs[kind], d, c),
+            piece(landings[kind], to, c),
+            send_sem.at[kind, d, c],
+            recv_sem.at[kind, to, c],
+            beside[d],
+        )
+
+    def first_leg(kind, d, c):
+        return remote(
+            piece(packs[kind], d, c),
+            relay_in.at[kind * chunks + c],
+            send_sem.at[kind, d, c],
+            relay_recv.at[kind, c],
+            beside[d ^ 1],
+        )
+
+    def second_leg(kind, d, c):
+        return remote(
+            relay_in.at[kind * chunks + c],
+            piece(landings[kind], d ^ 1, c),
+            relay_send.at[kind, c],
+            recv_sem.at[kind, d ^ 1, c],
+            two_on[d],
+        )
+
+    def send(kind, d, c):
+        relayed = by_relay[d][c]
+        if relayed is False:
+
+            @pl.when(inside[d])
+            def _():
+                direct(kind, d, c, d ^ 1).start()
+
+        else:
+
+            @pl.when(inside[d] & relayed)
+            def _():
+                first_leg(kind, d, c).start()
+
+            @pl.when(inside[d] & jnp.logical_not(relayed))
+            def _():
+                direct(kind, d, c, d ^ 1).start()
+
+    def pass_on(kind):
+        for c in range(chunks):
+            for d in range(nd):
+                if hands_on[d][c] is not False:
+
+                    @pl.when(hands_on[d][c])
+                    def _(c=c, d=d):
+                        first_leg(kind, d, c).wait_recv()
+                        second_leg(kind, d, c).start()
+
+    def arrived(kind):
+        pass_on(kind)
+        for d in range(nd):
+
+            @pl.when(inside[d])
+            def _(d=d):
+                for c in range(chunks):
+                    direct(kind, d, c, d).wait_recv()
 
     for kind, (full, pack) in enumerate(((k, k_pack), (v, v_pack))):
         loads[kind].wait()
@@ -162,12 +237,10 @@
             for s in range(cap):
                 pack[d * cap + s] = full[owed_head[d][s]]
         if kind == 0:
-            pl.semaphore_wait(barrier, sum(ok.astype(jnp.int32) for ok in inside))
-        for d in range(nd):
-
-            @pl.when(inside[d])
-            def _(kind=kind, d=d):
-                forward(kind, d, d ^ 1).start()
+            pl.semaphore_wait(barrier, sum(ok.astype(jnp.int32) for ok, _ in greeted))
+        for c in range(chunks):
+            for d in range(nd):
+                send(kind, d, c)
 
     read_head = [table(me, beside[d], inside[d], read_slot, d) for d in range(nd)]
     blank = jnp.zeros((rows, width), q.dtype)
@@ -184,13 +257,6 @@
 
     lax.fori_loop(0, heads, own_scores, 0)
 
-    def arrived(kind):
-        for d in range(nd):
-
-            @pl.when(inside[d])
-            def _(d=d):
-                forward(kind, d, d).wait_recv()
-
     arrived(0)
 
     def softmax(h, carry):
@@ -218,11 +284,8 @@
             h = read_head[d][s]
             part = dot_plain(p16[h * E + d + 1], g[h])
             vp_pack[d * cap + s] = part.astype(vp_pack.dtype)
-        for s in range(cap):
-
-            @pl.when(inside[d])
-            def _(d=d, s=s):
-                backward(0, d, s, d ^ 1).start()
+        for c in range(chunks):
+            send(2, d, c)
 
     arrived(1)
 
@@ -243,11 +306,8 @@
             h = read_head[d][s]
             part = dot_plain(s16[h * E + d + 1], q[h]) * scale
             kp_pack[d * cap + s] = part.astype(kp_pack.dtype)
-        for s in range(cap):
-
-            @pl.when(inside[d])
-            def _(d=d, s=s):
-                backward(1, d, s, d ^ 1).start()
+        for c in range(chunks):
+            send(3, d, c)
 
     def own_results(h, carry):
         slots = [read_slot[d * heads + h] for d in range(nd)]
@@ -267,12 +327,7 @@
     stores[1].start()
 
     for kind, total, terms, result in ((0, vg32, vp_in, vg), (1, kg32, kp_in, kg)):
-        for d in range(nd):
-
-            @pl.when(inside[d])
-            def _(kind=kind, d=d):
-                for s in range(cap):
-                    backward(kind, d, s, d).wait_recv()
+        arrived(2 + kind)
 
         def add_terms(h, carry, total=total, terms=terms, result=result):
             value = total[h]
@@ -284,14 +339,20 @@
         lax.fori_loop(0, heads, add_terms, 0)
         stores[2 + kind].start()
 
-    for kind in range(2):
+    for kind in range(4):
         for d in range(nd):
-
-            @pl.when(inside[d])
-            def _(kind=kind, d=d):
-                forward(kind, d, d ^ 1).wait_send()
-                for s in range(cap):
-                    backward(kind, d, s, d ^ 1).wait_send()
+            for c in range(chunks):
+
+                @pl.when(inside[d])
+                def _(kind=kind, d=d, c=c):
+                    direct(kind, d, c, d).wait_send()
+
+                if hands_on[d][c] is not False:
+
+                    @pl.when(hands_on[d][c])
+                    def _(kind=kind, d=d, c=c):
+                        second_leg(kind, d, c).wait_send()
+
     for store in stores:
         store.wait()
 
@@ -318,6 +379,7 @@
     cap = HCAP * max(1, heads // 6)
     nd = len(directions(tile_count))
     E = nd + 1
+    chunks = tile_count // 2 if nd == 2 else 1
     low = queries.dtype
     shape = jax.ShapeDtypeStruct(queries.shape, low)
     anywhere = pl.BlockSpec(memory_space=pl.ANY)
@@ -326,7 +388,7 @@
     landed = pltpu.VMEM((nd * cap + 1, rows, width), low)
     wide = pltpu.VMEM((heads, rows, width), jnp.float32)
     results = pl.pallas_call(
-        functools.partial(kernel, (tile_count, entries, cap)),
+        functools.partial(kernel, (tile_count, entries, cap, chunks)),
         out_shape=(shape,) * 4,
         in_specs=[pl.BlockSpec(memory_space=pltpu.SMEM)] + [anywhere] * 4,
         out_specs=(anywhere,) * 4,
@@ -347,10 +409,11 @@
             wide,
             pltpu.SMEM((nd * heads,), jnp.int32),
             pltpu.SMEM((nd * heads,), jnp.int32),
-            pltpu.SemaphoreType.DMA((2, nd)),
-            pltpu.SemaphoreType.DMA((2, nd)),
-            pltpu.SemaphoreType.DMA((2, nd * cap)),
-            pltpu.SemaphoreType.DMA((2, nd * cap)),
+            pltpu.VMEM((4 * chunks, cap, rows // chunks, width), low),
+            pltpu.SemaphoreType.DMA((4, nd, chunks)),
+            pltpu.SemaphoreType.DMA((4, nd, chunks)),
+            pltpu.SemaphoreType.DMA((4, chunks)),
+            pltpu.SemaphoreType.DMA((4, chunks)),
             pltpu.SemaphoreType.DMA((4,)),
             pltpu.SemaphoreType.DMA((4,)),
         ],

time: 42.8 us -> 42.2 us (0.986)
  Pallas kernels: 42 us -> 41.4 us
    pallas_call x1, Pallas kernels: 39.8 us -> 39.2 us  [per_device(): pl.pallas_call(functools.partial(kernel, (tile_count, entries, cap, chunk...]
where the time goes in v3:
time: 42.2 us; the launch traced here: 42 us
  Pallas kernels  41.4 us (98%)
  between operations  0.64 us (2%)
    pallas_call x1, Pallas kernels, per_device(): pl.pallas_call(functools.partial(kernel, (tile_count, entries, cap, chunk...  39.2 us
    pallas_call x1, Pallas kernels, per_device(): pl.pallas_call(write_results, out_shape=(shape,) * 4, in_specs=[anywhere]...  2.2 us

profile of v3, /device:TPU:18, one launch (start us, length us, event | category | flops | bytes accessed | tf_op | source)
XLA Modules:
  0.0 42.0 jit_solution(16363826702119408413)
XLA Ops:
  0.6 39.2 %tile_attention.1 = (bf16[6,256,128]{2,1,0:T(8,128)(2,1)}, bf16[6,256,128]{2,1,0:T(8,128)(2,1)}, bf16[6,256,128]{2,1,0:T(8,128)(2,1)}, bf16[6,256,128]{2,1,0:T(8,128)(2,1)}) custom-call(s32[6,4,8]{2,1,0:T(4,128)} %bitcast.1, bf16[6,256,128]{2,1,0:T(8,128)(2,1)} %q_hbm.1, bf16[6,256,128]{2,1,0:T(8,128)(2,1)} %k_hbm.1, bf16[6,256,128]{2,1,0:T(8,128)(2,1)} %v_hbm.1, ...), custom_call_target="tpu_custom_call" | custom-call | tf_op jit(solution)/shard_map/tile_attention/pallas_call | solution.py:390
  39.8 2.2 %write_results.1 = (bf16[6,256,128]{2,1,0:T(8,128)(2,1)}, bf16[6,256,128]{2,1,0:T(8,128)(2,1)}, bf16[6,256,128]{2,1,0:T(8,128)(2,1)}, bf16[6,256,128]{2,1,0:T(8,128)(2,1)}) custom-call(bf16[6,256,128]{2,1,0:T(8,128)(2,1)} %get-tuple-element.8.refs_0_, bf16[6,256,128]{2,1,0:T(8,128)(2,1)} %get-tuple-element.9.refs_1_, ...), custom_call_target="tpu_custom_call" | custom-call | tf_op jit(solution)/shard_map/write_results/pallas_call | solution.py:425

commit v4 on v3

--- a/solution.py
+++ b/solution.py
@@ -194,23 +194,21 @@
             two_on[d],
         )
 
-    def send(kind, d, c):
-        relayed = by_relay[d][c]
-        if relayed is False:
-
-            @pl.when(inside[d])
-            def _():
-                direct(kind, d, c, d ^ 1).start()
-
-        else:
-
-            @pl.when(inside[d] & relayed)
-            def _():
-                first_leg(kind, d, c).start()
-
-            @pl.when(inside[d] & jnp.logical_not(relayed))
-            def _():
-                direct(kind, d, c, d ^ 1).start()
+    def send(kind):
+        for c in range(chunks):
+            for d in range(nd):
+                if by_relay[d][c] is not False:
+
+                    @pl.when(inside[d] & by_relay[d][c])
+                    def _(c=c, d=d):
+                        first_leg(kind, d, c).start()
+
+        for c in range(chunks):
+            for d in range(nd):
+
+                @pl.when(inside[d] & jnp.logical_not(by_relay[d][c]))
+                def _(c=c, d=d):
+                    direct(kind, d, c, d ^ 1).start()
 
     def pass_on(kind):
         for c in range(chunks):
@@ -238,9 +236,7 @@
                 pack[d * cap + s] = full[owed_head[d][s]]
         if kind == 0:
             pl.semaphore_wait(barrier, sum(ok.astype(jnp.int32) for ok, _ in greeted))
-        for c in range(chunks):
-            for d in range(nd):
-                send(kind, d, c)
+        send(kind)
 
     read_head = [table(me, beside[d], inside[d], read_slot, d) for d in range(nd)]
     blank = jnp.zeros((rows, width), q.dtype)
@@ -284,8 +280,7 @@
             h = read_head[d][s]
             part = dot_plain(p16[h * E + d + 1], g[h])
             vp_pack[d * cap + s] = part.astype(vp_pack.dtype)
-        for c in range(chunks):
-            send(2, d, c)
+    send(2)
 
     arrived(1)
 
@@ -306,8 +301,7 @@
             h = read_head[d][s]
             part = dot_plain(s16[h * E + d + 1], q[h]) * scale
             kp_pack[d * cap + s] = part.astype(kp_pack.dtype)
-        for c in range(chunks):
-            send(3, d, c)
+    send(3)
 
     def own_results(h, carry):
         slots = [read_slot[d * heads + h] for d in range(nd)]

time: 42.2 us -> 40.3 us (0.955)
  the two profiles are of different devices: /device:TPU:18 before, /device:TPU:0 now
where the time goes in v4:
time: 40.3 us; the launch traced here: 40.1 us
  Pallas kernels  39.5 us (98%)
  between operations  0.64 us (2%)
    pallas_call x1, Pallas kernels, per_device(): pl.pallas_call(functools.partial(kernel, (tile_count, entries, cap, chunk...  37.3 us
    pallas_call x1, Pallas kernels, per_device(): pl.pallas_call(write_results, out_shape=(shape,) * 4, in_specs=[anywhere]...  2.2 us

profile of v4, /device:TPU:0, one launch (start us, length us, event | category | flops | bytes accessed | tf_op | source)
XLA Modules:
  0.0 40.1 jit_solution(4452435584944836301)
XLA Ops:
  0.6 37.3 %tile_attention.1 = (bf16[6,256,128]{2,1,0:T(8,128)(2,1)}, bf16[6,256,128]{2,1,0:T(8,128)(2,1)}, bf16[6,256,128]{2,1,0:T(8,128)(2,1)}, bf16[6,256,128]{2,1,0:T(8,128)(2,1)}) custom-call(s32[6,4,8]{2,1,0:T(4,128)} %bitcast.1, bf16[6,256,128]{2,1,0:T(8,128)(2,1)} %q_hbm.1, bf16[6,256,128]{2,1,0:T(8,128)(2,1)} %k_hbm.1, bf16[6,256,128]{2,1,0:T(8,128)(2,1)} %v_hbm.1, ...), custom_call_target="tpu_custom_call" | custom-call | tf_op jit(solution)/shard_map/tile_attention/pallas_call | solution.py:384
  37.9 2.2 %write_results.1 = (bf16[6,256,128]{2,1,0:T(8,128)(2,1)}, bf16[6,256,128]{2,1,0:T(8,128)(2,1)}, bf16[6,256,128]{2,1,0:T(8,128)(2,1)}, bf16[6,256,128]{2,1,0:T(8,128)(2,1)}) custom-call(bf16[6,256,128]{2,1,0:T(8,128)(2,1)} %get-tuple-element.8.refs_0_, bf16[6,256,128]{2,1,0:T(8,128)(2,1)} %get-tuple-element.9.refs_1_, ...), custom_call_target="tpu_custom_call" | custom-call | tf_op jit(solution)/shard_map/write_results/pallas_call | solution.py:419
